TPU v7x, 512 devices: a whole 4x8x8 slice. The times are simulated.
512 devices in a mesh: ctx: 64 (over z, x, y_lo), tp: 8 (over y_hi, core).
Axes of the slice: x: 4, y: 8 (y_hi: 4, y_lo: 2; y = y_hi * 2 + y_lo), z: 8, core: 2. Of those that a mesh axis runs over, the one named last changes fastest.
Arguments:
- tokens: bfloat16 [8192, 4096], P('ctx'), may hold values from -6 to 6
- new_token_states: bfloat16 [4, 4096], replicated, may hold values from -6.0625 to 6.0625
- w_query: bfloat16 [4096, 2048], P('ctx', 'tp'), may hold values from -0.12162204 to 0.12162204
- key_matrix: bfloat16 [4096, 1024], P('ctx', 'tp'), may hold values from -0.12162204 to 0.12162204
- value_matrix: bfloat16 [4096, 1024], P('ctx', 'tp'), may hold values from -0.09375 to 0.09375
- w_out: bfloat16 [2048, 4096], P('tp', 'ctx'), may hold values from -0.125 to 0.125
- lengths: int32 [4], replicated, may hold values from 1 to 4096, 8192 in all
- block_map: int32 [128], replicated, may hold values from 0 to 127, each once
Outputs:
- prefill_out: bfloat16 [8192, 4096], P('ctx', 'tp')
- decode_out: bfloat16 [4, 4096], P(None, 'tp')
Inputs may be any that keep to these rules, and one draw needn't show every extreme that they name: The lengths sum to 8192, and some request has exactly 4096 tokens. `block_map`: each of the 128 initial blocks is held exactly once.
All inputs are finite; a program needn't handle non-finite values.
Results may differ from a plain program's by a relative error of at most 0.015.
Values may be sent and summed in bfloat16 or wider, within the bound.
A program may use at most 64 MiB of HBM per device.

v0:
```python
import math
import jax
import jax.numpy as jnp
from jax import lax
from jax.sharding import PartitionSpec as P

HEAD_SIZE = 128
floor_value = -1e30


def initial_positions(block_map, first_row, row_count, block_rows):
    row_ids = first_row + jnp.arange(row_count, dtype=jnp.int32)
    block_ids = row_ids // block_rows
    table_ids = jnp.arange(block_map.shape[0], dtype=jnp.int32)
    mapped = jnp.sum(
        jnp.where(block_ids[:, None] == table_ids[None, :], block_map[None, :], 0), axis=1
    )
    return mapped * block_rows + row_ids % block_rows


def request_index(positions, request_ends):
    return jnp.sum((positions[:, None] >= request_ends[None, :]).astype(jnp.int32), axis=1)


def round_weights(weights):
    rounded = weights.astype(jnp.bfloat16)
    rounded = lax.optimization_barrier(rounded)
    return rounded.astype(jnp.float32)


def softmax_parts(
    dec_heads, projected_key_rows, projected_value_rows, owned, kv_heads, head_dim, score_scale
):
    row_count = projected_key_rows.shape[0]
    scores = (
        jnp.einsum(
            "rgjd,tgd->rgjt",
            dec_heads,
            projected_key_rows.reshape(row_count, kv_heads, head_dim),
            preferred_element_type=jnp.float32,
        )
        * score_scale
    )
    scores = jnp.where(owned, scores, floor_value)
    part_peak = jnp.max(scores, axis=3)
    weights = jnp.where(owned, jnp.exp(scores - part_peak[..., None]), 0.0)
    part_total = jnp.sum(weights, axis=3)
    part_mixed = jnp.einsum(
        "rgjt,tgd->rgjd",
        weights.astype(jnp.bfloat16),
        projected_value_rows.reshape(row_count, kv_heads, head_dim),
        preferred_element_type=jnp.float32,
    )
    return (part_peak, part_total, part_mixed)


def on_device(
    tokens, new_token_states, w_query, key_matrix, value_matrix, w_out, lengths, block_map
):
    local_rows = tokens.shape[0]
    block_rows = local_rows // 2
    request_count = new_token_states.shape[0]
    head_dim = HEAD_SIZE
    query_width = w_query.shape[1]
    kv_width = key_matrix.shape[1]
    kv_heads = kv_width // head_dim
    query_group_count = query_width // kv_width
    score_scale = 1.0 / math.sqrt(head_dim)
    device = lax.axis_index("ctx")
    request_ends = jnp.cumsum(lengths)
    inputs = jnp.concatenate([tokens, new_token_states], axis=0)
    shard_pieces = (
        lax.all_gather(w_query, "ctx", axis=0, tiled=True),
        lax.all_gather(key_matrix, "ctx", axis=0, tiled=True),
        lax.all_gather(value_matrix, "ctx", axis=0, tiled=True),
    )
    query_all, key_all, value_all = tuple(
        (jnp.dot(inputs, weight, preferred_element_type=jnp.float32) for weight in shard_pieces)
    )
    query_all = query_all.astype(jnp.bfloat16)
    key_all = key_all.astype(jnp.bfloat16)
    value_all = value_all.astype(jnp.bfloat16)
    local_query = query_all[:local_rows]
    local_keys = key_all[:local_rows]
    local_values = value_all[:local_rows]
    dec_query = query_all[local_rows:]
    decode_key_rows = key_all[local_rows:]
    decode_value_rows = value_all[local_rows:]
    token_pos = initial_positions(block_map, device * local_rows, local_rows, block_rows)
    token_request = request_index(token_pos, request_ends)
    query_heads = local_query.reshape(local_rows, kv_heads, query_group_count, head_dim)

    def attend(running, shard_pieces, first_row):
        peak_run, total_run, mixed_run = running
        key_piece, value_piece = shard_pieces
        row_count = key_piece.shape[0]
        key_pos = initial_positions(block_map, first_row, row_count, block_rows)
        key_request = request_index(key_pos, request_ends)
        allowed = (key_request[None, :] == token_request[:, None]) & (
            key_pos[None, :] <= token_pos[:, None]
        )
        scores = (
            jnp.einsum(
                "tgjd,kgd->gjtk",
                query_heads,
                key_piece.reshape(row_count, kv_heads, head_dim),
                preferred_element_type=jnp.float32,
            )
            * score_scale
        )
        scores = jnp.where(allowed, scores, floor_value)
        peak_new = jnp.maximum(peak_run, jnp.max(scores, axis=3))
        weights = jnp.where(allowed, jnp.exp(scores - peak_new[..., None]), 0.0)
        rescale = jnp.exp(peak_run - peak_new)
        total_new = total_run * rescale + jnp.sum(weights, axis=3)
        mixed_new = mixed_run * rescale[..., None] + jnp.einsum(
            "gjtk,kgd->gjtd",
            weights.astype(jnp.bfloat16),
            value_piece.reshape(row_count, kv_heads, head_dim),
            preferred_element_type=jnp.float32,
        )
        return (peak_new, total_new, mixed_new)

    start_state = (
        jnp.full((kv_heads, query_group_count, local_rows), floor_value, jnp.float32),
        jnp.zeros((kv_heads, query_group_count, local_rows), jnp.float32),
        jnp.zeros((kv_heads, query_group_count, local_rows, head_dim), jnp.float32),
    )
    dec_heads = dec_query.reshape(request_count, kv_heads, query_group_count, head_dim)
    request_ids = jnp.arange(request_count, dtype=jnp.int32)
    cache_keys, cache_values = (
        lax.all_gather(local_keys, "ctx", axis=0, tiled=True),
        lax.all_gather(local_values, "ctx", axis=0, tiled=True),
    )
    total_rows = cache_keys.shape[0]
    shard_count = total_rows // local_rows
    limit = max(1, 1024 // local_rows)
    step_rows = local_rows * math.gcd(shard_count, 1 << limit.bit_length() - 1)

    def key_step(running, step_index):
        first_row = step_index * step_rows
        pieces = (
            lax.dynamic_slice_in_dim(cache_keys, first_row, step_rows, 0),
            lax.dynamic_slice_in_dim(cache_values, first_row, step_rows, 0),
        )
        return (attend(running, pieces, first_row), None)

    final_state, unused = lax.scan(
        key_step, start_state, jnp.arange(total_rows // step_rows, dtype=jnp.int32)
    )
    peak_run, total_run, mixed_run = final_state
    cache_pos = (
        block_map[:, None] * block_rows + jnp.arange(block_rows, dtype=jnp.int32)[None, :]
    ).reshape(total_rows)
    cache_request = request_index(cache_pos, request_ends)
    owned = (cache_request[None, :] == request_ids[:, None])[:, None, None, :]
    cache_peak, cache_total, cache_mixed = softmax_parts(
        dec_heads, cache_keys, cache_values, owned, kv_heads, head_dim, score_scale
    )
    attended = (
        (mixed_run / total_run[..., None]).transpose(2, 0, 1, 3).reshape(local_rows, query_width)
    )
    attended = attended.astype(jnp.bfloat16)
    own_keys = decode_key_rows.reshape(request_count, kv_heads, 1, head_dim).astype(jnp.float32)
    own_values = decode_value_rows.reshape(request_count, kv_heads, 1, head_dim).astype(jnp.float32)
    self_scores = jnp.sum(dec_heads.astype(jnp.float32) * own_keys, axis=3) * score_scale
    peak_all = jnp.maximum(cache_peak, self_scores)
    rescale = jnp.exp(cache_peak - peak_all)
    self_weights = jnp.exp(self_scores - peak_all)
    dec_total = cache_total * rescale + self_weights
    dec_mixed = (
        cache_mixed * rescale[..., None] + round_weights(self_weights)[..., None] * own_values
    )
    dec_attn = (
        (dec_mixed / dec_total[..., None]).reshape(request_count, query_width).astype(jnp.bfloat16)
    )
    attended_all = jnp.concatenate([attended, dec_attn], axis=0)
    projected = jnp.dot(
        attended_all,
        lax.all_gather(w_out, "ctx", axis=1, tiled=True),
        preferred_element_type=jnp.float32,
    )
    summed_rows = lax.psum_scatter(
        projected.astype(jnp.bfloat16), "tp", scatter_dimension=1, tiled=True
    ).astype(jnp.float32)
    summed_rows = summed_rows.astype(jnp.bfloat16)
    return (summed_rows[:local_rows], summed_rows[local_rows:])


def solution(mesh):
    return jax.shard_map(
        on_device,
        mesh=mesh,
        in_specs=(
            P("ctx", None),
            P(),
            P("ctx", "tp"),
            P("ctx", "tp"),
            P("ctx", "tp"),
            P("tp", "ctx"),
            P(),
            P(),
        ),
        out_specs=(P("ctx", "tp"), P(None, "tp")),
        check_vma=False,
    )
```

profile of v0, /device:TPU:17, one launch (start us, length us, event | category | flops | bytes accessed | tf_op | source)
XLA Modules:
  0.0 1876.2 jit_solution(13340912142481138147)
XLA Ops:
  7.2 0.7 all-gather.7.cloned.1.call-update
  8.0 0.7 all-gather.13.cloned.1.call-update
  8.7 0.7 all-gather.11.cloned.1.call-update
  9.4 1.3 constant_dynamic-update-slice_fusion.1
  10.8 258.8 %all-gather.7.cloned.1.call-done = bf16[4096,128]{1,0:T(8,128)(2,1)} async-done(((bf16[64,128]{1,0:T(8,128)(2,1)}), bf16[4096,128]{1,0:T(8,128)(2,1)}) %all-gather.7.cloned.1.call-update) | async-done | bytes 1048592 | tf_op jit(solution)/shard_map/all_gather | solution.py:74
  269.6 1.7 convolution_convert_fusion.3
  271.2 0.6 slice.32
  271.9 296.3 %all-gather.13.cloned.1.call-done = bf16[4096,128]{1,0:T(8,128)(2,1)} async-done(((bf16[64,128]{1,0:T(8,128)(2,1)}), bf16[4096,128]{1,0:T(8,128)(2,1)}) %all-gather.13.cloned.1.call-update) | async-done | bytes 1048592 | tf_op jit(solution)/shard_map/all_gather | solution.py:75
  568.3 1.7 convolution_convert_fusion.2
  570.0 0.6 slice.34
  570.6 0.5 all-gather.17.cloned.1.call-update
  572.1 300.8 %all-gather.11.cloned.1.call-done = bf16[4096,256]{1,0:T(8,128)(2,1)} async-done(((bf16[64,256]{1,0:T(8,128)(2,1)}), bf16[4096,256]{1,0:T(8,128)(2,1)}) %all-gather.11.cloned.1.call-update) | async-done | bytes 2097168 | tf_op jit(solution)/shard_map/all_gather | solution.py:73
  872.9 2.1 convolution_convert_fusion.1
  875.2 300.6 %all-gather.9.cloned.1.call-done = bf16[8192,128]{1,0:T(8,128)(2,1)} async-done(((bf16[128,128]{1,0:T(8,128)(2,1)}), bf16[8192,128]{1,0:T(8,128)(2,1)}) %all-gather.9.cloned.1.call-update) | async-done | bytes 2097168 | tf_op jit(solution)/shard_map/all_gather | solution.py:132
  1175.8 302.3 %all-gather.15.cloned.1.call-done = bf16[8192,128]{1,0:T(8,128)(2,1)} async-done(((bf16[128,128]{1,0:T(8,128)(2,1)}), bf16[8192,128]{1,0:T(8,128)(2,1)}) %all-gather.15.cloned.1.call-update) | async-done | bytes 2097168 | tf_op jit(solution)/shard_map/all_gather | solution.py:133
  1478.1 40.4 %while.17 = (s32[]{:T(128)}, f32[1,2,128]{2,1,0:T(2,128)S(1)}, f32[1,2,128]{2,1,0:T(2,128)S(1)}, f32[1,2,128,128]{3,2,1,0:T(8,128)S(1)}, s32[8]{0:T(128)S(1)}, /...) while((s32[]{:T(128)}, f32[1,2,128]{2,1,0:T(2,128)S(1)}, ...), condition=%wide.region_8.9_spmd.clone, body=%wide.region_3.8_spmd.clone.sunk | while | flops 137504256 | bytes 4577019 | solution.py:148
  1478.1 0.6 dynamic_slice.37
  1479.3 0.4 select_reduce_fusion.3
  1479.8 0.3 compare_and_fusion.2
  1480.2 1.3 fusion.90
  1481.5 1.4 fusion.93
  1483.1 0.6 dynamic_slice.37
  1484.4 0.4 select_reduce_fusion.3
  1484.9 0.3 compare_and_fusion.2
  1485.2 1.3 fusion.90
  1486.5 1.4 fusion.93
  1488.2 0.6 dynamic_slice.37
  1489.4 0.4 select_reduce_fusion.3
  1489.9 0.3 compare_and_fusion.2
  1490.3 1.3 fusion.90
  1491.6 1.4 fusion.93
  1493.2 0.6 dynamic_slice.37
  1494.5 0.4 select_reduce_fusion.3
  1495.0 0.3 compare_and_fusion.2
  1495.3 1.3 fusion.90
  1496.6 1.4 fusion.93
  1498.3 0.6 dynamic_slice.37
  1499.5 0.4 select_reduce_fusion.3
  1500.0 0.3 compare_and_fusion.2
  1500.4 1.3 fusion.90
  1501.7 1.4 fusion.93
  1503.3 0.6 dynamic_slice.37
  1504.6 0.4 select_reduce_fusion.3
  1505.1 0.3 compare_and_fusion.2
  1505.4 1.3 fusion.90
  1506.7 1.4 fusion.93
  1508.4 0.6 dynamic_slice.37
  1509.6 0.4 select_reduce_fusion.3
  1510.1 0.3 compare_and_fusion.2
  1510.5 1.3 fusion.90
  1511.8 1.4 fusion.93
  1513.4 0.6 dynamic_slice.37
  1514.7 0.4 select_reduce_fusion.3
  1515.2 0.3 compare_and_fusion.2
  1515.5 1.3 fusion.90
  1516.8 1.4 fusion.93
  1518.5 2.5 fusion.72
  1521.0 0.3 fusion.51
  1521.3 0.5 fusion.48
  1522.1 258.3 %all-gather.17.cloned.1.call-done = bf16[256,4096]{0,1:T(8,128)(2,1)} async-done(((bf16[256,64]{0,1:T(8,128)(2,1)}), bf16[256,4096]{0,1:T(8,128)(2,1)}) %all-gather.17.cloned.1.call-update) | async-done | bytes 2097168 | tf_op jit(solution)/shard_map/all_gather | solution.py:180
  1780.4 3.4 convolution_convert_fusion
  1783.8 82.6 %reduce-scatter.2.cloned.1.call-done = bf16[132,512]{1,0:T(8,128)(2,1)} async-done(((bf16[132,4096]{1,0:T(8,128)(2,1)}), bf16[132,512]{1,0:T(8,128)(2,1)}) %reduce-scatter.2.cloned.1.call-update) | async-done | bytes 135184 | tf_op jit(solution)/shard_map/reduce_scatter | solution.py:183
  1866.5 1.6 slice.38
  1868.0 1.3 slice.39
  (104 shorter events, 4.6 us)
Async XLA Ops:
  7.2 3.6 copy-start
  7.2 262.4 %all-gather.7.cloned.1.call-start = ((), (), s32[]{:S(2)}) async-start(), calls=%async_computation.1 | async-start | bytes 1064960 | tf_op jit(solution)/shard_map/all_gather | solution.py:74
  7.9 560.4 %all-gather.13.cloned.1.call-start = ((), (), s32[]{:S(2)}) async-start(), calls=%async_computation.4 | async-start | bytes 1064960 | tf_op jit(solution)/shard_map/all_gather | solution.py:75
  8.7 864.2 %all-gather.11.cloned.1.call-start = ((), (), s32[]{:S(2)}) async-start(), calls=%async_computation.3 | async-start | bytes 2129920 | tf_op jit(solution)/shard_map/all_gather | solution.py:73
  9.4 1166.4 %all-gather.9.cloned.1.call-start = ((), (), s32[]{:S(2)}) async-start(), calls=%async_computation.2 | async-start | bytes 2129920 | tf_op jit(solution)/shard_map/all_gather | solution.py:132
  10.8 560.5 %copy-start.3 = (s32[4]{0:T(128)S(1)}, s32[4]{0:T(128)}, u32[]{:S(2)}) copy-start(s32[4]{0:T(128)} %param.16) | copy-start | bytes 52
  10.8 560.6 %copy-start.1 = (s32[128]{0:T(128)S(1)}, s32[128]{0:T(128)}, u32[]{:S(2)}) copy-start(s32[128]{0:T(128)} %param.17) | copy-start | bytes 1540
  271.9 1206.2 %all-gather.15.cloned.1.call-start = ((), (), s32[]{:S(2)}) async-start(), calls=%async_computation.5 | async-start | bytes 2129920 | tf_op jit(solution)/shard_map/all_gather | solution.py:133
  570.6 1209.8 %all-gather.17.cloned.1.call-start = ((), (), s32[]{:S(2)}) async-start(), calls=%async_computation.6 | async-start | bytes 2129920 | tf_op jit(solution)/shard_map/all_gather | solution.py:180
  571.2 1295.3 %reduce-scatter.2.cloned.1.call-start = ((), (), s32[]{:S(2)}) async-start(), calls=%async_computation.7 | async-start | bytes 1253376 | tf_op jit(solution)/shard_map/reduce_scatter | solution.py:183
  1518.5 2.8 copy-start.2
Sparse Core Ops, SparseCore 0:
  10.1 259.4 all-gather.6
  271.6 296.5 all-gather.12
  570.4 302.4 all-gather.10
  875.4 300.3 all-gather.8
  1177.7 300.3 all-gather.14
  1480.0 300.3 all-gather.16
  1783.9 82.4 reduce-scatter.1
where the time goes:
time: 1880 us
  waiting for transfers between devices  1800 us (96%)
  matrix products  33.2 us (2%)
    all_gather x1, waiting for transfers between devices, on_device(): lax.all_gather(local_values, 'ctx', axis=0, tiled=True)  302 us
    all_gather x1, waiting for transfers between devices, on_device(): lax.all_gather(w_query, 'ctx', axis=0, tiled=True)  301 us
    all_gather x1, waiting for transfers between devices, on_device(): lax.all_gather(local_keys, 'ctx', axis=0, tiled=True)  301 us
    all_gather x1, waiting for transfers between devices, on_device(): lax.all_gather(value_matrix, 'ctx', axis=0, tiled=True)  296 us
    all_gather x1, waiting for transfers between devices, on_device(): lax.all_gather(key_matrix, 'ctx', axis=0, tiled=True)  259 us
    all_gather x1, waiting for transfers between devices, on_device(): lax.all_gather(w_out, 'ctx', axis=1, tiled=True)  258 us
    reduce_scatter x1, waiting for transfers between devices, on_device(): lax.psum_scatter(projected.astype(jnp.bfloat16), 'tp', scatter_dimension=...  82.6 us
  transfers between devices with their start and end apart: 7, of which 7 were waited for; matrix products, arithmetic and copies ran while one was open for 3% of the time, Pallas kernels for 0%

commit v1 on v0

--- a/solution.py
+++ b/solution.py
@@ -69,9 +69,18 @@
     device = lax.axis_index("ctx")
     request_ends = jnp.cumsum(lengths)
     inputs = jnp.concatenate([tokens, new_token_states], axis=0)
+    keep_up_roots = lambda inner_x: jnp.concatenate(
+        jax.lax.all_to_all(
+            jnp.stack([inner_x] * jax.lax.psum(1, "ctx"), axis=0),
+            axis_name="ctx",
+            split_axis=0,
+            concat_axis=0,
+        ),
+        0,
+    )
     shard_pieces = (
         lax.all_gather(w_query, "ctx", axis=0, tiled=True),
-        lax.all_gather(key_matrix, "ctx", axis=0, tiled=True),
+        keep_up_roots(key_matrix),
         lax.all_gather(value_matrix, "ctx", axis=0, tiled=True),
     )
     query_all, key_all, value_all = tuple(

time: 1880 us -> 1580 us (0.84)
  waiting for transfers between devices: 1800 us -> 1490 us
    all_gather x1 -> x0, waiting for transfers between devices: 259 us -> none  [on_device(): lax.all_gather(key_matrix, 'ctx', axis=0, tiled=True)]
    all_gather x1, waiting for transfers between devices: 296 us -> 218 us  [on_device(): lax.all_gather(value_matrix, 'ctx', axis=0, tiled=True)]
    all_to_all x0 -> x1, waiting for transfers between devices: none -> 26.4 us  [on_device(): jax.lax.all_to_all(jnp.stack([inner_x] * jax.lax.psum(1, 'ctx'), axis=0),...]
where the time goes in v1:
time: 1580 us
  waiting for transfers between devices  1490 us (94%)
  matrix products  32.1 us (2%)
    all_gather x1, waiting for transfers between devices, on_device(): lax.all_gather(local_values, 'ctx', axis=0, tiled=True)  302 us
    all_gather x1, waiting for transfers between devices, on_device(): lax.all_gather(local_keys, 'ctx', axis=0, tiled=True)  301 us
    all_gather x1, waiting for transfers between devices, on_device(): lax.all_gather(w_query, 'ctx', axis=0, tiled=True)  300 us
    all_gather x1, waiting for transfers between devices, on_device(): lax.all_gather(w_out, 'ctx', axis=1, tiled=True)  258 us
    all_gather x1, waiting for transfers between devices, on_device(): lax.all_gather(value_matrix, 'ctx', axis=0, tiled=True)  218 us
    reduce_scatter x1, waiting for transfers between devices, on_device(): lax.psum_scatter(projected.astype(jnp.bfloat16), 'tp', scatter_dimension=...  82.5 us
  transfers between devices with their start and end apart: 7, of which 7 were waited for; matrix products, arithmetic and copies ran while one was open for 3% of the time, Pallas kernels for 0%

profile of v1, /device:TPU:17, one launch (start us, length us, event | category | flops | bytes accessed | tf_op | source)
XLA Modules:
  0.0 1578.3 jit_solution(1833813509447543973)
XLA Ops:
  7.2 0.7 all-gather.10.cloned.1.call-update
  8.0 0.7 all-gather.8.cloned.1.call-update
  8.7 2.0 stack.2
  10.6 14.6 all-to-all-start
  25.5 26.4 %all-to-all-done = bf16[64,64,128]{2,1,0:T(8,128)(2,1)S(1)} async-done(((bf16[64,64,128]{2,1,0:T(8,128)(2,1)}), bf16[64,64,128]{2,1,0:T(8,128)(2,1)S(1)}, u32[]{:S(2)}, u32[]{:S(2)}) %all-to-all-start) | async-done | bytes 1048608 | tf_op jit(solution)/shard_map/all_to_all | solution.py:73
  51.9 0.5 convolution_convert_fusion.3
  52.3 0.6 slice.32
  53.0 218.1 %all-gather.10.cloned.1.call-done = bf16[4096,128]{1,0:T(8,128)(2,1)} async-done(((bf16[64,128]{1,0:T(8,128)(2,1)}), bf16[4096,128]{1,0:T(8,128)(2,1)}) %all-gather.10.cloned.1.call-update) | async-done | bytes 1048592 | tf_op jit(solution)/shard_map/all_gather | solution.py:84
  271.1 1.7 convolution_convert_fusion.2
  272.8 0.6 slice.34
  273.5 0.5 all-gather.14.cloned.1.call-update
  275.0 299.8 %all-gather.8.cloned.1.call-done = bf16[4096,256]{1,0:T(8,128)(2,1)} async-done(((bf16[64,256]{1,0:T(8,128)(2,1)}), bf16[4096,256]{1,0:T(8,128)(2,1)}) %all-gather.8.cloned.1.call-update) | async-done | bytes 2097168 | tf_op jit(solution)/shard_map/all_gather | solution.py:82
  574.8 2.1 convolution_convert_fusion.1
  577.2 300.7 %all-gather.6.cloned.1.call-done = bf16[8192,128]{1,0:T(8,128)(2,1)} async-done(((bf16[128,128]{1,0:T(8,128)(2,1)}), bf16[8192,128]{1,0:T(8,128)(2,1)}) %all-gather.6.cloned.1.call-update) | async-done | bytes 2097168 | tf_op jit(solution)/shard_map/all_gather | solution.py:141
  877.9 302.3 %all-gather.12.cloned.1.call-done = bf16[8192,128]{1,0:T(8,128)(2,1)} async-done(((bf16[128,128]{1,0:T(8,128)(2,1)}), bf16[8192,128]{1,0:T(8,128)(2,1)}) %all-gather.12.cloned.1.call-update) | async-done | bytes 2097168 | tf_op jit(solution)/shard_map/all_gather | solution.py:142
  1180.2 40.4 %while.17 = (s32[]{:T(128)}, f32[1,2,128]{2,1,0:T(2,128)S(1)}, f32[1,2,128]{2,1,0:T(2,128)S(1)}, f32[1,2,128,128]{3,2,1,0:T(8,128)S(1)}, s32[8]{0:T(128)S(1)}, /...) while((s32[]{:T(128)}, f32[1,2,128]{2,1,0:T(2,128)S(1)}, ...), condition=%wide.region_8.9_spmd.clone, body=%wide.region_3.8_spmd.clone.sunk | while | flops 137504256 | bytes 4577019 | solution.py:157
  1180.2 0.6 dynamic_slice.37
  1181.4 0.4 select_reduce_fusion.3
  1181.9 0.3 compare_and_fusion.2
  1182.3 1.3 fusion.90
  1183.6 1.4 fusion.93
  1185.2 0.6 dynamic_slice.37
  1186.5 0.4 select_reduce_fusion.3
  1187.0 0.3 compare_and_fusion.2
  1187.3 1.3 fusion.90
  1188.6 1.4 fusion.93
  1190.3 0.6 dynamic_slice.37
  1191.5 0.4 select_reduce_fusion.3
  1192.0 0.3 compare_and_fusion.2
  1192.4 1.3 fusion.90
  1193.7 1.4 fusion.93
  1195.3 0.6 dynamic_slice.37
  1196.6 0.4 select_reduce_fusion.3
  1197.1 0.3 compare_and_fusion.2
  1197.4 1.3 fusion.90
  1198.7 1.4 fusion.93
  1200.4 0.6 dynamic_slice.37
  1201.7 0.4 select_reduce_fusion.3
  1202.1 0.3 compare_and_fusion.2
  1202.5 1.3 fusion.90
  1203.8 1.4 fusion.93
  1205.4 0.6 dynamic_slice.37
  1206.7 0.4 select_reduce_fusion.3
  1207.2 0.3 compare_and_fusion.2
  1207.5 1.3 fusion.90
  1208.8 1.4 fusion.93
  1210.5 0.6 dynamic_slice.37
  1211.8 0.4 select_reduce_fusion.3
  1212.2 0.3 compare_and_fusion.2
  1212.6 1.3 fusion.90
  1213.9 1.4 fusion.93
  1215.6 0.6 dynamic_slice.37
  1216.8 0.4 select_reduce_fusion.3
  1217.3 0.3 compare_and_fusion.2
  1217.6 1.3 fusion.90
  1219.0 1.4 fusion.93
  1220.6 2.5 fusion.72
  1223.1 0.3 fusion.51
  1223.4 0.5 fusion.48
  1224.2 258.4 %all-gather.14.cloned.1.call-done = bf16[256,4096]{0,1:T(8,128)(2,1)} async-done(((bf16[256,64]{0,1:T(8,128)(2,1)}), bf16[256,4096]{0,1:T(8,128)(2,1)}) %all-gather.14.cloned.1.call-update) | async-done | bytes 2097168 | tf_op jit(solution)/shard_map/all_gather | solution.py:189
  1482.6 3.4 convolution_convert_fusion
  1486.1 82.5 %reduce-scatter.2.cloned.1.call-done = bf16[132,512]{1,0:T(8,128)(2,1)} async-done(((bf16[132,4096]{1,0:T(8,128)(2,1)}), bf16[132,512]{1,0:T(8,128)(2,1)}) %reduce-scatter.2.cloned.1.call-update) | async-done | bytes 135184 | tf_op jit(solution)/shard_map/reduce_scatter | solution.py:192
  1568.6 1.6 slice.38
  1570.2 1.3 slice.39
  (106 shorter events, 4.7 us)
Async XLA Ops:
  7.2 18.2 %copy-start = (bf16[128,4096]{1,0:T(8,128)(2,1)S(1)}, bf16[128,4096]{1,0:T(8,128)(2,1)}, u32[]{:S(2)}) copy-start(bf16[128,4096]{1,0:T(8,128)(2,1)} %param.10) | copy-start | bytes 3145732
  7.2 263.9 %all-gather.10.cloned.1.call-start = ((), (), s32[]{:S(2)}) async-start(), calls=%async_computation.4 | async-start | bytes 1064960 | tf_op jit(solution)/shard_map/all_gather | solution.py:84
  7.9 566.9 %all-gather.8.cloned.1.call-start = ((), (), s32[]{:S(2)}) async-start(), calls=%async_computation.3 | async-start | bytes 2129920 | tf_op jit(solution)/shard_map/all_gather | solution.py:82
  10.6 14.8 copy-start.1
  10.6 41.3 %all-to-all-start = ((bf16[64,64,128]{2,1,0:T(8,128)(2,1)}), bf16[64,64,128]{2,1,0:T(8,128)(2,1)S(1)}, u32[]{:S(2)}, u32[]{:S(2)}) async-start(bf16[64,64,128]{2,1,0:T(8,128)(2,1)} %stack.2), calls=%async_computation | async-start | bytes 2097152 | tf_op jit(solution)/shard_map/all_to_all | solution.py:73
  25.3 852.6 %all-gather.6.cloned.1.call-start = ((), (), s32[]{:S(2)}) async-start(), calls=%async_computation.2 | async-start | bytes 2129920 | tf_op jit(solution)/shard_map/all_gather | solution.py:141
  51.9 222.3 %copy-start.4 = (s32[4]{0:T(128)S(1)}, s32[4]{0:T(128)}, u32[]{:S(2)}) copy-start(s32[4]{0:T(128)} %param.16) | copy-start | bytes 52
  51.9 222.4 %copy-start.2 = (s32[128]{0:T(128)S(1)}, s32[128]{0:T(128)}, u32[]{:S(2)}) copy-start(s32[128]{0:T(128)} %param.17) | copy-start | bytes 1540
  53.0 1127.2 %all-gather.12.cloned.1.call-start = ((), (), s32[]{:S(2)}) async-start(), calls=%async_computation.5 | async-start | bytes 2129920 | tf_op jit(solution)/shard_map/all_gather | solution.py:142
  273.5 1209.2 %all-gather.14.cloned.1.call-start = ((), (), s32[]{:S(2)}) async-start(), calls=%async_computation.6 | async-start | bytes 2129920 | tf_op jit(solution)/shard_map/all_gather | solution.py:189
  274.0 1294.5 %reduce-scatter.2.cloned.1.call-start = ((), (), s32[]{:S(2)}) async-start(), calls=%async_computation.7 | async-start | bytes 1253376 | tf_op jit(solution)/shard_map/reduce_scatter | solution.py:192
  1220.6 2.8 copy-start.3
Sparse Core Ops, SparseCore 0:
  10.1 260.9 all-gather.9
  273.2 301.5 all-gather.7
  577.5 300.3 all-gather.5
  879.8 300.3 all-gather.11
  1182.1 300.4 all-gather.13
  1486.2 82.3 reduce-scatter.1
